TPU v7x, 32 devices: a whole 2x2x4 slice. The times are simulated.
32 devices in a mesh: grp: 4 (over x, core), blk: 8 (over z, y).
Axes of the slice: x: 2, y: 2, z: 4, core: 2. Of those that a mesh axis runs over, the one named last changes fastest.
Arguments:
- pair_density: bfloat16 [2048, 8192], P('grp', 'blk'), may hold values from -14 to 14
- energies: float32 [2048], P('grp'), may hold values from 1 to 4
- batch_live: int32 [4], replicated, may hold values from 1 to 512, 1280 in all
- coulomb_root: float32 [8192], replicated, may hold values from 0.5 to 2
Outputs:
- polarized: bfloat16 [4, 8192, 8192], P('grp', 'blk')
- screened: float32 [4, 8192, 128], P('grp', 'blk')
Inputs may be any that keep to these rules, and one draw needn't show every extreme that they name: Group g's live transitions are its first batch_live[g] slots of 512; at least one group is full.
All inputs are finite; a program needn't handle non-finite values.
Results may differ from a plain program's by a relative error of at most 0.03.
Values may be sent and summed in bfloat16 or wider, within the bound.
A program may use at most 128 MiB of HBM per device.

v0:
```python
import math

import jax
import jax.numpy as jnp
from jax import lax
from jax.sharding import PartitionSpec as P

G = 8192
CW = 128
DYSON = 2


def live_weights(all_energy, batch_live, slots, total_slots, group_ids, frequencies, norm_factor):
    positions = jnp.arange(total_slots, dtype=jnp.int32)
    owner_match = (positions // slots)[:, None] == group_ids[None, :]
    limits = jnp.sum(jnp.where(owner_match, batch_live[None, :], 0), axis=1)
    is_live = (positions % slots < limits).astype(jnp.float32)
    weight = (
        -2.0
        * all_energy[None, :]
        / (all_energy[None, :] * all_energy[None, :] + frequencies[:, None] * frequencies[:, None])
    )
    return weight * is_live[None, :] * norm_factor


def body(pair_density, energies, batch_live, coulomb_root):
    slots = pair_density.shape[0]
    width_own = pair_density.shape[1]
    group_count = lax.axis_size("grp")
    block_count = lax.axis_size("blk")
    total_slots = slots * group_count
    group_index = lax.axis_index("grp")
    block_index = lax.axis_index("blk")
    norm_factor = 1.0 / math.sqrt(total_slots)
    own_root = lax.dynamic_slice_in_dim(coulomb_root, block_index * width_own, width_own)
    group_ids = jnp.arange(group_count, dtype=jnp.int32)
    row_density, all_energy = (
        lax.all_gather(pair_density, "grp", axis=0, tiled=True),
        lax.all_gather(energies.astype(jnp.bfloat16), "grp", axis=0, tiled=True).astype(
            energies.dtype
        ),
    )
    frequencies = 0.6 * jnp.arange(group_count, dtype=jnp.float32)
    weight = live_weights(
        all_energy, batch_live, slots, total_slots, group_ids, frequencies, norm_factor
    )
    scaled = (weight[:, :, None] * row_density.astype(jnp.float32)[None, :, :]).astype(jnp.bfloat16)
    sub_width = width_own // group_count
    my_slice = lax.dynamic_slice_in_dim(row_density, group_index * sub_width, sub_width, 1)
    root_table = jnp.reshape(coulomb_root, (block_count, group_count, sub_width))
    my_roots = jnp.reshape(
        lax.dynamic_index_in_dim(root_table, group_index, 1, keepdims=False), (-1,)
    )
    chi = jnp.einsum(
        "ftc,tk->fck",
        scaled,
        lax.all_gather(my_slice, "blk", axis=1, tiled=True),
        preferred_element_type=jnp.float32,
    )
    quarter = own_root[None, :, None] * chi * my_roots[None, None, :]
    received = lax.all_to_all(
        quarter.astype(jnp.bfloat16), "grp", split_axis=0, concat_axis=0, tiled=True
    )
    received = jnp.reshape(received, (group_count, width_own, block_count, sub_width))
    polarized = jnp.reshape(
        jnp.transpose(received, (1, 2, 0, 3)), (width_own, width_own * block_count)
    )
    lead_blocks = (CW + width_own - 1) // width_own
    lead = quarter[:, :, : lead_blocks * sub_width]
    lead_back = lax.all_to_all(
        lead.astype(jnp.bfloat16), "grp", split_axis=0, concat_axis=0, tiled=True
    ).astype(lead.dtype)
    lead_back = jnp.reshape(lead_back, (group_count, width_own, lead_blocks, sub_width))
    window = jnp.reshape(
        jnp.transpose(lead_back, (1, 2, 0, 3)), (width_own, lead_blocks * width_own)
    )[:, :CW]
    state = window
    for dyson_step in range(DYSON):
        rounded = state.astype(jnp.bfloat16)
        product = jnp.dot(
            polarized,
            lax.all_gather(rounded, "blk", axis=0, tiled=True),
            preferred_element_type=jnp.float32,
        )
        state = window + 8.0 / G * product
    return (polarized[None], state[None])


def solution(mesh):
    placed = (P("grp", "blk"), P("grp"), P(), P())
    return jax.shard_map(
        body,
        mesh=mesh,
        in_specs=placed,
        out_specs=(P("grp", "blk", None), P("grp", "blk", None)),
        check_vma=False,
    )
```

profile of v0, /device:TPU:0, one launch (start us, length us, event | category | flops | bytes accessed | tf_op | source)
XLA Modules:
  0.0 552.5 jit_solution(9522642114145184739)
XLA Ops:
  7.2 0.0 all-gather.6.cloned.1.call-start
  7.2 0.7 all-gather.6.cloned.1.call-update
  7.9 0.0 all-gather.8.cloned.1.call-start
  8.0 38.8 %all-gather.6.cloned.1.call-done = bf16[2048,1024]{1,0:T(8,128)(2,1)} async-done(((bf16[512,1024]{1,0:T(8,128)(2,1)}), bf16[2048,1024]{1,0:T(8,128)(2,1)}) %all-gather.6.cloned.1.call-update) | async-done | bytes 4194320 | tf_op jit(solution)/shard_map/all_gather | solution.py:38
  46.7 2.3 constant_dynamic-slice_fusion
  49.0 0.0 all-gather.8.cloned.1.call-update
  49.0 0.7 convert_element_type.28
  49.7 0.8 reshape.112
  50.5 0.7 dynamic_slice.10
  51.2 5.2 all-gather
  56.4 0.8 select_reduce_fusion
  57.2 0.1 multiply_multiply_fusion
  57.3 7.3 %copy.18 = f32[2048,1024]{0,1:T(8,128)} copy(bf16[2048,1024]{1,0:T(8,128)(2,1)} %all-gather.6.cloned.1.call-done) | data formatting | bytes 12582912 | tf_op jit(solution)/shard_map/convert_element_type | solution.py:47
  64.6 109.7 %all-gather.8.cloned.1.call-done = bf16[2048,2048]{1,0:T(8,128)(2,1)} async-done(((bf16[2048,256]{1,0:T(8,128)(2,1)}), bf16[2048,2048]{1,0:T(8,128)(2,1)}) %all-gather.8.cloned.1.call-update) | async-done | bytes 8388624 | tf_op jit(solution)/shard_map/all_gather | solution.py:57
  174.3 42.5 %multiply_convert_fusion = bf16[4,1024,2048]{2,1,0:T(8,128)(2,1)} fusion(f32[2048]{0:T(1024)S(1)} %bitcast.33, f32[2048,1024]{0,1:T(8,128)} %copy.18, f32[4,2048]{1,0:T(4,128)S(1)} %multiply_multiply_fusion, f32[1024]{0:T(1024)S(1)} %dynamic_slice.10, bf16[2048,2048]{1,0:T(8,128)(2,1)} %all-gather.8.cloned.1.call-done), kind=kOutput, calls=%fused_computation | convolution fusion | flops 34401681408 | bytes 33599488 | tf_op jit(solution)/shard_map/ftc,tk->fck/dot_general | solution.py:54
  216.8 1.7 slice.13
  218.5 28.2 %all_to_all.10 = bf16[4,1024,256]{2,1,0:T(8,128)(2,1)S(1)} all-to-all(bf16[4,1024,256]{2,1,0:T(8,128)(2,1)S(1)} %slice.13), channel_id=1, replica_groups=mesh['grp'=4,'blk'=8] {'grp'}, dimensions={0} | all-to-all | bytes 4194304 | tf_op jit(solution)/shard_map/all_to_all | solution.py:70
  246.8 7.0 %all-to-all-start = ((bf16[4,1024,2048]{2,1,0:T(8,128)(2,1)}), bf16[4,1024,2048]{2,1,0:T(8,128)(2,1)}, u32[]{:S(2)}, u32[]{:S(2)}) async-start(bf16[4,1024,2048]{2,1,0:T(8,128)(2,1)} %multiply_convert_fusion), calls=%async_computation | async-start | bytes 33554432 | tf_op jit(solution)/shard_map/all_to_all | solution.py:61
  253.8 0.0 all-gather.10.cloned.1.call-start
  253.8 2.5 copy.20
  256.4 1.0 slice.14
  257.3 0.8 copy.23
  258.2 0.0 all-gather.10.cloned.1.call-update
  258.2 0.2 all-gather.12.cloned.1.call-start
  258.4 178.4 %all-to-all-done = bf16[4,1024,2048]{2,1,0:T(8,128)(2,1)} async-done(((bf16[4,1024,2048]{2,1,0:T(8,128)(2,1)}), bf16[4,1024,2048]{2,1,0:T(8,128)(2,1)}, u32[]{:S(2)}, u32[]{:S(2)}) %all-to-all-start) | async-done | bytes 16777248 | tf_op jit(solution)/shard_map/all_to_all | solution.py:61
  436.8 16.3 %copy.24 = bf16[512,8,8,256]{3,2,1,0:T(8,128)(2,1)} copy(bf16[512,8,8,256]{3,1,2,0:T(8,128)(2,1)} %bitcast.15) | data formatting | bytes 33554432
  453.0 0.0 copy-start
  453.0 23.2 %copy.19 = bf16[4,1024,8,256]{1,3,0,2:T(8,128)(2,1)} copy(bf16[4,1024,8,256]{3,2,1,0:T(8,128)(2,1)} %bitcast.28) | data formatting | bytes 33554432 | tf_op jit(solution)/shard_map/reshape | solution.py:64
  476.2 0.0 all-gather.10.cloned.1.call-done
  476.2 0.0 copy-done
  476.2 11.6 %fusion.6 = bf16[1024,128]{1,0:T(8,128)(2,1)} fusion(bf16[1024,8192]{0,1:T(8,128)(2,1)} %bitcast.25, bf16[8192,128]{1,0:T(8,128)(2,1)} %all-gather.10.cloned.1.call-done, bf16[1024,128]{1,0:T(8,128)(2,1)S(1)} %copy-done), kind=kOutput, calls=%fused_computation.10 | convolution fusion | flops 2148007936 | bytes 19398656 | tf_op jit(solution)/shard_map/dot_general | solution.py:80
  487.8 0.0 all-gather.12.cloned.1.call-update
  487.9 21.3 %copy.22 = bf16[1,1024,8192]{2,1,0:T(8,128)(2,1)} copy(bf16[1,1024,8192]{1,2,0:T(8,128)(2,1)} %bitcast.26) | data formatting | bytes 33554432
  509.1 25.2 %all-gather.12.cloned.1.call-done = bf16[8192,128]{1,0:T(8,128)(2,1)} async-done(((bf16[1024,128]{1,0:T(8,128)(2,1)}), bf16[8192,128]{1,0:T(8,128)(2,1)}) %all-gather.12.cloned.1.call-update) | async-done | bytes 2097168 | tf_op jit(solution)/shard_map/all_gather | solution.py:82
  534.3 11.7 %fusion.5 = f32[1,1024,128]{2,1,0:T(8,128)} fusion(bf16[1024,8192]{0,1:T(8,128)(2,1)} %bitcast.27, bf16[8192,128]{1,0:T(8,128)(2,1)} %all-gather.12.cloned.1.call-done, bf16[1024,128]{1,0:T(8,128)(2,1)S(1)} %copy-done), kind=kOutput, calls=%fused_computation.9 | convolution fusion | flops 2147876864 | bytes 19660800 | tf_op jit(solution)/shard_map/dot_general | solution.py:80
  (6 shorter events, 0.1 us)
Async XLA Ops:
  7.2 39.6 %all-gather.6.cloned.1.call-start = ((), (), s32[]{:S(2)}) async-start(), calls=%async_computation.2 | async-start | bytes 5242880 | tf_op jit(solution)/shard_map/all_gather | solution.py:38
  7.9 166.4 %all-gather.8.cloned.1.call-start = ((), (), s32[]{:S(2)}) async-start(), calls=%async_computation.3 | async-start | bytes 9437184 | tf_op jit(solution)/shard_map/all_gather | solution.py:57
  246.8 190.0 %all-to-all-start = ((bf16[4,1024,2048]{2,1,0:T(8,128)(2,1)}), bf16[4,1024,2048]{2,1,0:T(8,128)(2,1)}, u32[]{:S(2)}, u32[]{:S(2)}) async-start(bf16[4,1024,2048]{2,1,0:T(8,128)(2,1)} %multiply_convert_fusion), calls=%async_computation | async-start | bytes 33554432 | tf_op jit(solution)/shard_map/all_to_all | solution.py:61
  253.8 222.5 %all-gather.10.cloned.1.call-start = ((), (), s32[]{:S(2)}) async-start(), calls=%async_computation.4 | async-start | bytes 2359296 | tf_op jit(solution)/shard_map/all_gather | solution.py:82
  258.2 276.1 %all-gather.12.cloned.1.call-start = ((), (), s32[]{:S(2)}) async-start(), calls=%async_computation.5 | async-start | bytes 2359296 | tf_op jit(solution)/shard_map/all_gather | solution.py:82
  453.0 23.2 %copy-start = (bf16[1024,128]{1,0:T(8,128)(2,1)S(1)}, bf16[1024,128]{1,0:T(8,128)(2,1)}, u32[]{:S(2)}) copy-start(bf16[1024,128]{1,0:T(8,128)(2,1)} %copy.23) | copy-start | bytes 786436
Sparse Core Ops, SparseCore 0:
  9.5 37.1 all-gather.5
  49.4 124.9 all-gather.7
  258.3 47.6 all-gather.9
  488.0 46.2 all-gather.11
where the time goes:
time: 554 us; the launch traced here: 553 us
  waiting for transfers between devices  353 us (64%)
  local copies, waits for them, and re-layouts  77.9 us (14%)
  matrix products  65.7 us (12%)
  blocking collectives  33.4 us (6%)
  between operations  13.8 us (2%)
  starting transfers between devices  7.32 us (1%)
    all_to_all x1, waiting for transfers between devices, body(): lax.all_to_all(quarter.astype(jnp.bfloat16), 'grp', split_axis=0, concat_...  178 us
    all_gather x1, waiting for transfers between devices, body(): lax.all_gather(my_slice, 'blk', axis=1, tiled=True)  110 us
    dot_general x1, matrix products, body(): jnp.einsum('ftc,tk->fck', scaled, lax.all_gather(my_slice, 'blk', axis=1,...  42.5 us
    all_gather x1, waiting for transfers between devices, body(): lax.all_gather(pair_density, 'grp', axis=0, tiled=True)  38.8 us
    unnamed x6, local copies, waits for them, and re-layouts  38.4 us
    all_to_all x1, blocking collectives, body(): lax.all_to_all(lead.astype(jnp.bfloat16), 'grp', split_axis=0, concat_axi...  28.2 us
    all_gather x2, waiting for transfers between devices, body(): lax.all_gather(rounded, 'blk', axis=0, tiled=True)  25.2 us
    dot_general x2, matrix products, body(): jnp.dot(polarized, lax.all_gather(rounded, 'blk', axis=0, tiled=True), pr...  23.3 us
  transfers between devices with their start and end apart: 5, of which 4 were waited for; matrix products, arithmetic and copies ran while one was open for 14% of the time, Pallas kernels for 0%

commit v1 on v0

--- a/solution.py
+++ b/solution.py
@@ -1,13 +1,17 @@
+import functools
 import math
 
 import jax
 import jax.numpy as jnp
 from jax import lax
+from jax.experimental import pallas as pl
+from jax.experimental.pallas import tpu as pltpu
 from jax.sharding import PartitionSpec as P
 
 G = 8192
 CW = 128
 DYSON = 2
+LANES = 128
 
 
 def live_weights(all_energy, batch_live, slots, total_slots, group_ids, frequencies, norm_factor):
@@ -23,7 +27,7 @@
     return weight * is_live[None, :] * norm_factor
 
 
-def body(pair_density, energies, batch_live, coulomb_root):
+def plain_body(pair_density, energies, batch_live, coulomb_root):
     slots = pair_density.shape[0]
     width_own = pair_density.shape[1]
     group_count = lax.axis_size("grp")
@@ -86,10 +90,130 @@
     return (polarized[None], state[None])
 
 
+def pack_rows(batch_live, slots, total, packed):
+    ends = jnp.cumsum(batch_live)
+    starts = ends - batch_live
+    j = jnp.arange(packed, dtype=jnp.int32)
+    in_group = (j[:, None] >= starts[None, :]) & (j[:, None] < ends[None, :])
+    group_base = jnp.arange(batch_live.shape[0], dtype=jnp.int32) * slots - starts
+    source = jnp.sum(jnp.where(in_group, group_base[None, :] + j[:, None], 0), axis=1)
+    used = jnp.any(in_group, axis=1)
+    source = jnp.where(used, source, -1)
+    return source, used
+
+
+def chi_kernel(n, factor, a_ref, p_ref, w_ref, r_ref, out_ref, s_ref, at_ref, q_ref, u_ref, v_ref):
+    i = pl.program_id(0)
+    width = a_ref.shape[0]
+    last = (((1,), (1,)), ((), ()))
+    piece = p_ref[0, 0]
+    root = r_ref[...]
+
+    @pl.when(i == 0)
+    def _():
+        at_ref[:width] = a_ref[...]
+        lead = p_ref[0, 0, :, :CW].astype(jnp.float32) * root[:, :CW]
+        q = lead.T
+        q_ref[...] = q
+        at_ref[width:] = (q * w_ref[...]).astype(jnp.bfloat16)
+        u_ref[...] = jnp.zeros_like(u_ref)
+
+    @pl.when(i < n)
+    def _():
+        prod = jnp.dot(at_ref[...], piece, preferred_element_type=jnp.float32) * root
+        out_ref[...] = prod[:width].astype(jnp.bfloat16)
+        u_ref[...] += lax.dot_general(
+            (prod[width:] * root).astype(jnp.bfloat16), piece, last,
+            preferred_element_type=jnp.float32)
+
+    @pl.when(i == n - 1)
+    def _():
+        v_ref[...] = (u_ref[...] * (w_ref[...] * factor)).astype(jnp.bfloat16)
+
+    @pl.when(i >= n)
+    def _():
+        prod = jnp.dot(v_ref[...], piece, preferred_element_type=jnp.float32)
+        u_ref[...] += lax.dot_general(
+            (prod * (root * root)).astype(jnp.bfloat16), piece, last,
+            preferred_element_type=jnp.float32)
+
+    @pl.when(i == 2 * n - 1)
+    def _():
+        x = (q_ref[...] + factor * u_ref[...]).astype(jnp.bfloat16)
+        s_ref[...] = lax.dot_general(a_ref[...], x, last, preferred_element_type=jnp.float32)
+
+
+def chi_and_screen(left, pieces, weight, coulomb_root):
+    width, packed = left.shape
+    split, blocks, _, sub = pieces.shape
+    n = split * blocks
+    return pl.pallas_call(
+        functools.partial(chi_kernel, n, 8.0 / G),
+        grid=(2 * n,),
+        out_shape=(
+            jax.ShapeDtypeStruct((width, n * sub), jnp.bfloat16),
+            jax.ShapeDtypeStruct((width, CW), jnp.float32),
+        ),
+        in_specs=[
+            pl.BlockSpec((width, packed), lambda i: (0, 0)),
+            pl.BlockSpec((1, 1, packed, sub), lambda i: (i % split, (i // split) % blocks, 0, 0)),
+            pl.BlockSpec((1, packed), lambda i: (0, 0)),
+            pl.BlockSpec((1, sub), lambda i: (0, i % n)),
+        ],
+        out_specs=(
+            pl.BlockSpec((width, sub), lambda i: (0, jnp.minimum(i, n - 1))),
+            pl.BlockSpec((width, CW), lambda i: (0, 0)),
+        ),
+        scratch_shapes=[
+            pltpu.VMEM((width + CW, packed), jnp.bfloat16),
+            pltpu.VMEM((CW, packed), jnp.float32),
+            pltpu.VMEM((CW, packed), jnp.float32),
+            pltpu.VMEM((CW, packed), jnp.bfloat16),
+        ],
+        compiler_params=pltpu.CompilerParams(vmem_limit_bytes=48 * 1024 * 1024),
+    )(left, pieces, weight[None, :], coulomb_root[None, :])
+
+
+def gather_pieces(own, group_index, group_count, blocks):
+    sub = own.shape[1] // group_count
+    mine = lax.dynamic_slice_in_dim(own, group_index * sub, sub, 1)
+    row = lax.all_gather(mine, "blk", axis=0, tiled=False)
+    return lax.all_gather(row, "grp", axis=0, tiled=False)
+
+
+def body(pair_density, energies, batch_live, coulomb_root):
+    slots, width = pair_density.shape
+    group_count = lax.axis_size("grp")
+    blocks = lax.axis_size("blk")
+    total = slots * group_count
+    packed = total * 5 // 8
+    group_index = lax.axis_index("grp")
+    block_index = lax.axis_index("blk")
+    own_root = lax.dynamic_slice_in_dim(coulomb_root, block_index * width, width)
+
+    rows = lax.all_gather(pair_density, "grp", axis=0, tiled=True)
+    all_energy = lax.all_gather(energies, "grp", axis=0, tiled=True)
+    source, used = pack_rows(batch_live, slots, total, packed)
+    pick = source[:, None] == jnp.arange(total, dtype=jnp.int32)[None, :]
+    own = jnp.dot(pick.astype(jnp.bfloat16), rows, preferred_element_type=jnp.float32).astype(
+        jnp.bfloat16
+    )
+    energy = jnp.sum(jnp.where(pick, all_energy[None, :], 0.0), axis=1)
+    energy = jnp.where(used, energy, 1.0)
+    frequency = 0.6 * group_index.astype(jnp.float32)
+    weight = -2.0 * energy / (energy * energy + frequency * frequency)
+    weight = jnp.where(used, weight, 0.0) * (1.0 / math.sqrt(total))
+    left = (own.T.astype(jnp.float32) * weight[None, :] * own_root[:, None]).astype(jnp.bfloat16)
+    pieces = gather_pieces(own, group_index, group_count, blocks)
+    polarized, screened = chi_and_screen(left, pieces, weight, coulomb_root)
+    return (polarized[None], screened[None])
+
+
 def solution(mesh):
     placed = (P("grp", "blk"), P("grp"), P(), P())
+    aligned = (G // mesh.shape["blk"]) % (LANES * mesh.shape["grp"]) == 0
     return jax.shard_map(
-        body,
+        body if aligned else plain_body,
         mesh=mesh,
         in_specs=placed,
         out_specs=(P("grp", "blk", None), P("grp", "blk", None)),

time: 554 us -> 373 us (0.67)
  waiting for transfers between devices: 353 us -> 243 us
  Pallas kernels: 0 us -> 84.2 us
  local copies, waits for them, and re-layouts: 77.9 us -> 11 us
  matrix products: 65.7 us -> 8.39 us
  blocking collectives: 33.4 us -> 5.18 us
  starting transfers between devices: 7.32 us -> 0.12 us
    all_to_all x1 -> x0, waiting for transfers between devices: 178 us -> none  [body(): lax.all_to_all(quarter.astype(jnp.bfloat16), 'grp', split_axis=0, concat_...]
    pallas_call x0 -> x1, Pallas kernels: none -> 84.2 us  [chi_and_screen(): pl.pallas_call(functools.partial(chi_kernel, n, 8.0 / G), grid=(2 * n,),...]
    all_gather x4 -> x3, waiting for transfers between devices: 174 us -> 243 us  [the longest x1 120 us: gather_pieces(): return lax.all_gather(row, 'grp', axis=0, tiled=False)]
    dot_general x3 -> x1, matrix products: 65.7 us -> 8.39 us  [body(): jnp.dot(pick.astype(jnp.bfloat16), rows, preferred_element_type=jnp.float32)]
    unnamed x6, local copies, waits for them, and re-layouts: 38.4 us -> 2.25 us
    all_to_all x1 -> x0, blocking collectives: 28.2 us -> none  [body(): lax.all_to_all(lead.astype(jnp.bfloat16), 'grp', split_axis=0, concat_axi...]
    reshape x2 -> x0, local copies, waits for them, and re-layouts: 24 us -> none  [the longest x1 23.2 us: body(): jnp.reshape(received, (group_count, width_own, block_count, sub_width))]
    all_gather x0 -> x1, local copies, waits for them, and re-layouts: none -> 7.9 us  [gather_pieces(): row = lax.all_gather(mine, 'blk', axis=0, tiled=False)]
  transfers between devices with their start and end apart: 5 -> 3, of which waited for: 4 -> 3; matrix products, arithmetic and copies ran while one was open for 14% -> 2% of each run, Pallas kernels for 0% -> 0%
where the time goes in v1:
time: 373 us; the launch traced here: 372 us
  waiting for transfers between devices  243 us (65%)
  Pallas kernels  84.2 us (23%)
  between operations  13.8 us (4%)
  local copies, waits for them, and re-layouts  11 us (3%)
  matrix products  8.39 us (2%)
  other arithmetic  6.24 us (2%)
  blocking collectives  5.18 us (1%)
    all_gather x1, waiting for transfers between devices, gather_pieces(): return lax.all_gather(row, 'grp', axis=0, tiled=False)  120 us
    all_gather x1, waiting for transfers between devices, gather_pieces(): row = lax.all_gather(mine, 'blk', axis=0, tiled=False)  85.6 us
    pallas_call x1, Pallas kernels, chi_and_screen(): pl.pallas_call(functools.partial(chi_kernel, n, 8.0 / G), grid=(2 * n,),...  84.2 us
    all_gather x1, waiting for transfers between devices, body(): rows = lax.all_gather(pair_density, 'grp', axis=0, tiled=True)  37.1 us
    dot_general x1, matrix products, body(): jnp.dot(pick.astype(jnp.bfloat16), rows, preferred_element_type=jnp.float32)  8.39 us
    all_gather x1, local copies, waits for them, and re-layouts, gather_pieces(): row = lax.all_gather(mine, 'blk', axis=0, tiled=False)  7.9 us
  transfers between devices with their start and end apart: 3, of which 3 were waited for; matrix products, arithmetic and copies ran while one was open for 2% of the time, Pallas kernels for 0%

profile of v1, /device:TPU:0, one launch (start us, length us, event | category | flops | bytes accessed | tf_op | source)
XLA Modules:
  0.0 372.3 jit_solution(15246804766653983003)
XLA Ops:
  7.2 0.0 all-gather.7.cloned.1.call-start
  7.2 0.7 all-gather.7.cloned.1.call-update
  7.9 0.0 all-gather.9.cloned.1.call-start
  7.9 0.8 reduce-window.8
  8.8 0.7 multiply_subtract_fusion
  9.4 0.1 fusion.6
  9.5 0.1 select_reduce_fusion.1
  9.6 37.1 %all-gather.7.cloned.1.call-done = bf16[2048,1024]{1,0:T(8,128)(2,1)} async-done(((bf16[512,1024]{1,0:T(8,128)(2,1)}), bf16[2048,1024]{1,0:T(8,128)(2,1)}) %all-gather.7.cloned.1.call-update) | async-done | bytes 4194320 | tf_op jit(solution)/shard_map/all_gather | solution.py:194
  46.7 8.4 %fusion.2 = bf16[1280,1024]{0,1:T(8,128)(2,1)S(1)} fusion(bf16[2048,1024]{1,0:T(8,128)(2,1)} %all-gather.7.cloned.1.call-done, s32[1280]{0:T(1024)S(1)} %broadcast_select_fusion), kind=kOutput, calls=%fused_computation.5 | convolution fusion | flops 5372641280 | bytes 6820864 | tf_op jit(solution)/shard_map/dot_general | solution.py:198
  55.1 0.0 copy-start.1
  55.2 1.5 copy-done.1
  56.7 0.9 constant_dynamic-slice_fusion
  57.6 0.0 all-gather.9.cloned.1.call-update
  57.6 0.0 all-gather.11.cloned.1.call-start
  57.6 85.6 %all-gather.9.cloned.1.call-done = bf16[10240,256]{0,1:T(8,128)(2,1)} async-done(((bf16[1280,256]{0,1:T(8,128)(2,1)}), bf16[10240,256]{0,1:T(8,128)(2,1)}) %all-gather.9.cloned.1.call-update) | async-done | bytes 5242896 | tf_op jit(solution)/shard_map/all_gather | solution.py:180
  143.2 7.9 %copy.13 = bf16[10240,256]{1,0:T(8,128)(2,1)} copy(bf16[10240,256]{0,1:T(8,128)(2,1)} %all-gather.9.cloned.1.call-done) | data formatting | bytes 10485760 | tf_op jit(solution)/shard_map/all_gather | solution.py:180
  151.1 0.0 copy-start
  151.1 0.0 copy-start.2
  151.1 0.0 all-gather.11.cloned.1.call-update
  151.2 0.7 copy-done
  151.9 0.0 copy-done.2
  151.9 5.2 %all-gather.2 = f32[4,1,512]{2,1,0:T(1,128)S(1)} all-gather(f32[1,1,512]{2,1,0:T(1,128)S(1)} %bitcast.20), channel_id=1, replica_groups=mesh['grp'=4,'blk'=8] {'grp'}, dimensions={0}, use_global_device_ids=true | all-gather | bytes 10240 | tf_op jit(solution)/shard_map/all_gather | solution.py:195
  157.1 1.5 select_reduce_fusion
  158.6 3.0 fusion.3.a_ref
  161.6 119.9 %all-gather.11.cloned.1.call-done = bf16[32,1280,256]{2,1,0:T(8,128)(2,1)} async-done(((bf16[8,1280,256]{2,1,0:T(8,128)(2,1)}), bf16[32,1280,256]{2,1,0:T(8,128)(2,1)}) %all-gather.11.cloned.1.call-update) | async-done | bytes 20971536 | tf_op jit(solution)/shard_map/all_gather | solution.py:181
  281.5 84.2 %shard_map.59 = (bf16[1024,8192]{1,0:T(8,128)(2,1)}, f32[1024,128]{1,0:T(8,128)}) custom-call(bf16[1024,1280]{1,0:T(8,128)(2,1)S(1)} %fusion.3.a_ref, bf16[4,8,1280,256]{3,2,1,0:T(8,128)(2,1)} %bitcast.15, f32[1,1280]{1,0:T(1,128)S(1)} %fusion.5.w_ref, f32[1,8192]{1,0:T(1,128)S(1)} %bitcast.14), custom_call_target="tpu_custom_call" | custom-call | tf_op jit(solution)/shard_map/pallas_call | solution.py:150
  (4 shorter events, 0.1 us)
Async XLA Ops:
  7.2 39.6 %all-gather.7.cloned.1.call-start = ((), (), s32[]{:S(2)}) async-start(), calls=%async_computation | async-start | bytes 5242880 | tf_op jit(solution)/shard_map/all_gather | solution.py:194
  7.9 135.3 %all-gather.9.cloned.1.call-start = ((), (), s32[]{:S(2)}) async-start(), calls=%async_computation.1 | async-start | bytes 5898240 | tf_op jit(solution)/shard_map/all_gather | solution.py:180
  55.1 1.5 copy-start.1
  57.6 224.0 %all-gather.11.cloned.1.call-start = ((), (), s32[]{:S(2)}) async-start(), calls=%async_computation.2 | async-start | bytes 26214400 | tf_op jit(solution)/shard_map/all_gather | solution.py:181
  151.1 0.8 copy-start
  151.1 0.8 copy-start.2
Sparse Core Ops, SparseCore 0:
  9.5 37.1 all-gather.6
  57.7 85.4 all-gather.8
  151.3 130.1 all-gather.10

commit v2 on v1

--- a/solution.py
+++ b/solution.py
@@ -174,11 +174,183 @@
     )(left, pieces, weight[None, :], coulomb_root[None, :])
 
 
-def gather_pieces(own, group_index, group_count, blocks):
-    sub = own.shape[1] // group_count
-    mine = lax.dynamic_slice_in_dim(own, group_index * sub, sub, 1)
-    row = lax.all_gather(mine, "blk", axis=0, tiled=False)
-    return lax.all_gather(row, "grp", axis=0, tiled=False)
+def gather_kernel(nz, own_ref, out_ref, recv, s_up, s_down, s_y, s_x, s_pair, s_own):
+    g, b = lax.axis_index("grp"), lax.axis_index("blk")
+    x, c = g // 2, g % 2
+    z, y = b // 2, b % 2
+    half = own_ref.shape[1] // 2
+    rows = pl.ds(pl.multiple_of(c * half, half), half)
+    other_rows = pl.ds(pl.multiple_of((1 - c) * half, half), half)
+    to_up, to_down = (g, b + 2), (g, b - 2)
+    to_y = (g, z * 2 + 1 - y)
+    to_x = ((1 - x) * 2 + c, b)
+    to_pair = (x * 2 + 1 - c, b)
+    has_up, has_down = z + 1 < nz, z >= 1
+    skip_y, own_x = 2 * (1 - x), 2 * x
+
+    def copy(q, bb, sem, to, own=False):
+        src = own_ref.at[q, rows] if own else out_ref.at[q, bb, rows]
+        return pltpu.make_async_remote_copy(
+            src_ref=src, dst_ref=out_ref.at[q, bb, rows], send_sem=sem,
+            recv_sem=recv.at[q, bb, c], device_id=to, device_id_type=pl.DeviceIdType.MESH)
+
+    def arrived(q, bb):
+        copy(q, bb, s_pair.at[q, bb], to_pair).wait_recv()
+
+    def up(zz, j, own=False):
+        return copy(x + j, zz * 2 + y, s_up.at[j, zz], to_up, own)
+
+    def down(zz, j, own=False):
+        return copy(x + j, zz * 2 + y, s_down.at[j, zz], to_down, own)
+
+    def over_y(zz, j, own=False):
+        return copy(x + j, zz * 2 + y, s_y.at[j, zz], to_y, own)
+
+    def over_x(zz, yy, j):
+        return copy(x + j, zz * 2 + yy, s_x.at[j, zz * 2 + yy], to_x)
+
+    def over_pair(q, bb):
+        return copy(q, bb, s_pair.at[q, bb], to_pair)
+
+    def takes_y(zz, j):
+        return (zz % 2 == 0) | (j != skip_y)
+
+    def other_y_takes_x(zz, j):
+        return ((zz % 2 == 0) & (j == own_x)) | ((zz % 2 == 1) & (j != skip_y))
+
+    def when(condition, make, act):
+        @pl.when(condition)
+        def _():
+            getattr(make(), act)()
+
+    def from_z(zz, j, below, valid):
+        @pl.when(valid)
+        def _():
+            q, bb = x + j, zz * 2 + y
+            arrived(q, bb)
+            if below:
+                when(has_up, lambda: up(zz, j), "start")
+            else:
+                when(has_down, lambda: down(zz, j), "start")
+            when(takes_y(zz, j), lambda: over_y(zz, j), "start")
+            when(j == own_x, lambda: over_x(zz, y, j), "start")
+            over_pair(q, bb).start()
+
+    def from_y(zz, j, valid):
+        @pl.when(valid & takes_y(zz, j))
+        def _():
+            q, bb = x + j, zz * 2 + 1 - y
+            arrived(q, bb)
+            when(other_y_takes_x(zz, j), lambda: over_x(zz, 1 - y, j), "start")
+            over_pair(q, bb).start()
+
+    def from_x(zz, same_y, valid):
+        bb = zz * 2 + (y if same_y else 1 - y)
+
+        def take(q):
+            arrived(q, bb)
+            over_pair(q, bb).start()
+
+        if same_y:
+            @pl.when(valid)
+            def _():
+                take(3 * (1 - x))
+        else:
+            @pl.when(valid & (zz % 2 == 0))
+            def _():
+                take(3 * (1 - x))
+
+            @pl.when(valid & (zz % 2 == 1))
+            def _():
+                take(2 * (1 - x))
+                take(2 * (1 - x) + 1)
+
+    def at_distance(d):
+        if d == 0:
+            return [(z, True, z >= 0)]
+        return [(z - d, True, z >= d), (z + d, False, z + d < nz)]
+
+    barrier = pltpu.get_barrier_semaphore()
+
+    def greet(to):
+        pl.semaphore_signal(barrier, inc=1, device_id=to, device_id_type=pl.DeviceIdType.MESH)
+
+    for to in (to_y, to_x, to_pair):
+        greet(to)
+    pl.when(has_up)(lambda: greet(to_up))
+    pl.when(has_down)(lambda: greet(to_down))
+    peers = 3 + has_up.astype(jnp.int32) + has_down.astype(jnp.int32)
+    pl.semaphore_wait(barrier, peers)
+
+    for j in range(3):
+        when(has_up, lambda: up(z, j, True), "start")
+        when(has_down, lambda: down(z, j, True), "start")
+        when(takes_y(z, j), lambda: over_y(z, j, True), "start")
+    keep = pltpu.make_async_copy(own_ref, out_ref.at[:, b], s_own)
+    keep.start()
+
+    for s in range(nz + 1):
+        for j in range(3):
+            if 1 <= s + 1 < nz:
+                for zz, below, valid in at_distance(s + 1):
+                    from_z(zz, j, below, valid)
+            if s < nz:
+                for zz, _, valid in at_distance(s):
+                    from_y(zz, j, valid)
+        if 1 <= s < nz:
+            for zz, _, valid in at_distance(s):
+                from_x(zz, True, valid)
+        if s >= 1:
+            for zz, _, valid in at_distance(s - 1):
+                from_x(zz, False, valid)
+
+    def from_pair(q, bb):
+        pltpu.make_async_remote_copy(
+            src_ref=out_ref.at[q, bb, other_rows], dst_ref=out_ref.at[q, bb, other_rows],
+            send_sem=s_pair.at[q, bb], recv_sem=recv.at[q, bb, 1 - c],
+            device_id=to_pair, device_id_type=pl.DeviceIdType.MESH).wait_recv()
+        over_pair(q, bb).wait_send()
+
+    keep.wait()
+    for j in range(3):
+        when(has_up, lambda: up(z, j, True), "wait_send")
+        when(has_down, lambda: down(z, j, True), "wait_send")
+        when(takes_y(z, j), lambda: over_y(z, j, True), "wait_send")
+    for d in range(nz):
+        for zz, below, valid in at_distance(d):
+            for j in range(3):
+                if d >= 1:
+                    if below:
+                        when(valid & has_up, lambda: up(zz, j), "wait_send")
+                    else:
+                        when(valid & has_down, lambda: down(zz, j), "wait_send")
+                    when(valid & takes_y(zz, j), lambda: over_y(zz, j), "wait_send")
+                    when(valid & (j == own_x), lambda: over_x(zz, y, j), "wait_send")
+                when(valid & other_y_takes_x(zz, j), lambda: over_x(zz, 1 - y, j), "wait_send")
+            for same_y in (True, False):
+                if d >= 1 or not same_y:
+                    for q in range(4):
+                        pl.when(valid)(
+                            lambda q=q: from_pair(q, zz * 2 + (y if same_y else 1 - y)))
+
+
+def gather_pieces(own, blocks):
+    split, packed, sub = own.shape
+    nz = blocks // 2
+    dma = pltpu.SemaphoreType.DMA
+    sent = 28 * packed * sub
+    return pl.pallas_call(
+        functools.partial(gather_kernel, nz),
+        out_shape=jax.ShapeDtypeStruct((split, blocks, packed, sub), own.dtype),
+        in_specs=[pl.BlockSpec(memory_space=pltpu.VMEM)],
+        out_specs=pl.BlockSpec(memory_space=pl.ANY),
+        scratch_shapes=[
+            dma((split, blocks, 2)), dma((3, nz)), dma((3, nz)), dma((3, nz)),
+            dma((3, blocks)), dma((split, blocks)), dma(()),
+        ],
+        compiler_params=pltpu.CompilerParams(collective_id=0, has_side_effects=True),
+        cost_estimate=pl.CostEstimate(flops=0, bytes_accessed=2 * sent, transcendentals=0),
+    )(own)
 
 
 def body(pair_density, energies, batch_live, coulomb_root):
@@ -204,14 +376,20 @@
     weight = -2.0 * energy / (energy * energy + frequency * frequency)
     weight = jnp.where(used, weight, 0.0) * (1.0 / math.sqrt(total))
     left = (own.T.astype(jnp.float32) * weight[None, :] * own_root[:, None]).astype(jnp.bfloat16)
-    pieces = gather_pieces(own, group_index, group_count, blocks)
+    quarters = jnp.transpose(
+        jnp.reshape(own, (packed, group_count, width // group_count)), (1, 0, 2))
+    pieces = gather_pieces(quarters, blocks)
     polarized, screened = chi_and_screen(left, pieces, weight, coulomb_root)
     return (polarized[None], screened[None])
 
 
 def solution(mesh):
     placed = (P("grp", "blk"), P("grp"), P(), P())
-    aligned = (G // mesh.shape["blk"]) % (LANES * mesh.shape["grp"]) == 0
+    aligned = (
+        mesh.shape["grp"] == 4
+        and mesh.shape["blk"] % 2 == 0
+        and (G // mesh.shape["blk"]) % (LANES * mesh.shape["grp"]) == 0
+    )
     return jax.shard_map(
         body if aligned else plain_body,
         mesh=mesh,

time: 373 us -> 251 us (0.67)
  waiting for transfers between devices: 243 us -> 30 us
  Pallas kernels: 84.2 us -> 185 us
  local copies, waits for them, and re-layouts: 11 us -> 2.68 us
    all_gather x2 -> x0, waiting for transfers between devices: 205 us -> none  [the longest x1 120 us: gather_pieces(): return lax.all_gather(row, 'grp', axis=0, tiled=False)]
    pallas_call x0 -> x1, Pallas kernels: none -> 101 us  [gather_pieces(): pl.pallas_call(functools.partial(gather_kernel, nz), out_shape=jax.ShapeD...]
    all_gather x1 -> x0, local copies, waits for them, and re-layouts: 7.9 us -> none  [gather_pieces(): row = lax.all_gather(mine, 'blk', axis=0, tiled=False)]
    all_gather x1, waiting for transfers between devices: 37.1 us -> 29.3 us  [body(): rows = lax.all_gather(pair_density, 'grp', axis=0, tiled=True)]
  transfers between devices with their start and end apart: 3 -> 1, of which waited for: 3 -> 1; matrix products, arithmetic and copies ran while one was open for 2% -> 1% of each run, Pallas kernels for 0% -> 0%
where the time goes in v2:
time: 251 us
  Pallas kernels  185 us (74%)
  waiting for transfers between devices  30 us (12%)
  between operations  14.1 us (6%)
  matrix products  8.4 us (3%)
  blocking collectives  6.32 us (3%)
  other arithmetic  3.83 us (2%)
  local copies, waits for them, and re-layouts  2.68 us (1%)
    pallas_call x1, Pallas kernels, gather_pieces(): pl.pallas_call(functools.partial(gather_kernel, nz), out_shape=jax.ShapeD...  101 us
    pallas_call x1, Pallas kernels, chi_and_screen(): pl.pallas_call(functools.partial(chi_kernel, n, 8.0 / G), grid=(2 * n,),...  84.2 us
    all_gather x1, waiting for transfers between devices, body(): rows = lax.all_gather(pair_density, 'grp', axis=0, tiled=True)  29.3 us
    dot_general x1, matrix products, body(): jnp.dot(pick.astype(jnp.bfloat16), rows, preferred_element_type=jnp.float32)  8.4 us
    all_gather x1, blocking collectives, body(): all_energy = lax.all_gather(energies, 'grp', axis=0, tiled=True)  6.32 us
  transfers between devices with their start and end apart: 1, of which 1 were waited for; matrix products, arithmetic and copies ran while one was open for 1% of the time, Pallas kernels for 0%

profile of v2, /device:TPU:0, one launch (start us, length us, event | category | flops | bytes accessed | tf_op | source)
XLA Modules:
  0.0 250.6 jit_solution(11526063978431961514)
XLA Ops:
  7.2 0.0 all-gather.3.cloned.1.call-start
  7.2 0.7 all-gather.3.cloned.1.call-update
  7.9 0.8 reduce-window.8
  8.7 6.3 %all-gather = f32[4,1,512]{2,1,0:T(1,128)S(1)} all-gather(f32[1,1,512]{2,1,0:T(1,128)} %bitcast.20), channel_id=1, replica_groups=mesh['grp'=4,'blk'=8] {'grp'}, dimensions={0}, use_global_device_ids=true | all-gather | bytes 10240 | tf_op jit(solution)/shard_map/all_gather | solution.py:367
  15.1 0.7 multiply_subtract_fusion
  15.7 0.1 fusion.6
  15.8 0.1 select_reduce_fusion.1
  15.9 1.5 select_reduce_fusion
  17.4 29.3 %all-gather.3.cloned.1.call-done = bf16[2048,1024]{1,0:T(8,128)(2,1)} async-done(((bf16[512,1024]{1,0:T(8,128)(2,1)}), bf16[2048,1024]{1,0:T(8,128)(2,1)}) %all-gather.3.cloned.1.call-update) | async-done | bytes 4194320 | tf_op jit(solution)/shard_map/all_gather | solution.py:366
  46.7 8.4 %fusion.2 = bf16[1280,1024]{0,1:T(8,128)(2,1)S(1)} fusion(bf16[2048,1024]{1,0:T(8,128)(2,1)} %all-gather.3.cloned.1.call-done, s32[1280]{0:T(1024)S(1)} %broadcast_select_fusion), kind=kOutput, calls=%fused_computation.5 | convolution fusion | flops 5372641280 | bytes 6820864 | tf_op jit(solution)/shard_map/dot_general | solution.py:370
  55.1 2.6 %copy.8 = bf16[1280,4,256]{2,0,1:T(8,128)(2,1)} copy(bf16[1280,4,256]{0,2,1:T(8,128)(2,1)S(1)} %bitcast.15) | data formatting | bytes 5242880 | tf_op jit(solution)/shard_map/reshape | solution.py:380
  57.7 0.0 dynamic-slice-start
  57.7 101.1 %shard_map.59.p_ref = bf16[4,8,1280,256]{3,2,1,0:T(8,128)(2,1)} custom-call(bf16[4,1280,256]{2,1,0:T(8,128)(2,1)} %bitcast.16), custom_call_target="tpu_custom_call" | custom-call | bytes 18350080 | tf_op jit(solution)/shard_map/pallas_call | solution.py:342
  158.8 0.0 dynamic-slice-done
  158.8 0.0 copy-start
  158.8 0.6 fusion.3.a_ref
  159.4 0.1 copy-done
  159.6 84.2 %shard_map.60 = (bf16[1024,8192]{1,0:T(8,128)(2,1)}, f32[1024,128]{1,0:T(8,128)}) custom-call(bf16[1024,1280]{1,0:T(8,128)(2,1)S(1)} %fusion.3.a_ref, bf16[4,8,1280,256]{3,2,1,0:T(8,128)(2,1)} %shard_map.59.p_ref, f32[1,1280]{1,0:T(1,128)S(1)} %fusion.5.w_ref, f32[1,8192]{1,0:T(1,128)S(1)} %bitcast.14), custom_call_target="tpu_custom_call" | custom-call | tf_op jit(solution)/shard_map/pallas_call | solution.py:150
  (3 shorter events, 0.0 us)
Async XLA Ops:
  7.2 39.6 %all-gather.3.cloned.1.call-start = ((), (), s32[]{:S(2)}) async-start(), calls=%async_computation | async-start | bytes 5242880 | tf_op jit(solution)/shard_map/all_gather | solution.py:366
  57.7 101.1 %dynamic-slice-start = ((f32[8192]{0:T(1024)}, s32[]{:T(128)}), f32[1024]{0:T(1024)S(1)}, s32[]{:S(2)}) async-start(f32[8192]{0:T(1024)} %param.7, s32[]{:T(128)} %select_n.51), calls=%async_computation.1 | async-start | bytes 8704 | tf_op jit(solution)/shard_map/dynamic_slice | solution.py:364
  158.8 0.8 copy-start
Sparse Core Ops, SparseCore 0:
  9.5 37.1 all-gather.2

commit v3 on v2

--- a/solution.py
+++ b/solution.py
@@ -105,76 +105,82 @@
 def chi_kernel(n, factor, a_ref, p_ref, w_ref, r_ref, out_ref, s_ref, at_ref, q_ref, u_ref, v_ref):
     i = pl.program_id(0)
     width = a_ref.shape[0]
-    last = (((1,), (1,)), ((), ()))
-    piece = p_ref[0, 0]
-    root = r_ref[...]
+    split, _, _, sub = p_ref.shape
+
+    def root(k):
+        return r_ref[:, k * sub:(k + 1) * sub]
+
+    def spread(k, part):
+        part = (part * root(k)).T.astype(jnp.bfloat16)
+        return jnp.dot(p_ref[k, 0], part, preferred_element_type=jnp.float32)
 
     @pl.when(i == 0)
     def _():
         at_ref[:width] = a_ref[...]
-        lead = p_ref[0, 0, :, :CW].astype(jnp.float32) * root[:, :CW]
-        q = lead.T
+        q = (p_ref[0, 0, :, :CW].astype(jnp.float32) * r_ref[:, :CW]).T
         q_ref[...] = q
         at_ref[width:] = (q * w_ref[...]).astype(jnp.bfloat16)
         u_ref[...] = jnp.zeros_like(u_ref)
 
     @pl.when(i < n)
     def _():
-        prod = jnp.dot(at_ref[...], piece, preferred_element_type=jnp.float32) * root
-        out_ref[...] = prod[:width].astype(jnp.bfloat16)
-        u_ref[...] += lax.dot_general(
-            (prod[width:] * root).astype(jnp.bfloat16), piece, last,
-            preferred_element_type=jnp.float32)
+        for k in range(split):
+            prod = jnp.dot(at_ref[...], p_ref[k, 0], preferred_element_type=jnp.float32) * root(k)
+            out_ref[:, k * sub:(k + 1) * sub] = prod[:width].astype(jnp.bfloat16)
+            u_ref[...] += spread(k, prod[width:])
 
     @pl.when(i == n - 1)
     def _():
-        v_ref[...] = (u_ref[...] * (w_ref[...] * factor)).astype(jnp.bfloat16)
+        v_ref[...] = (u_ref[...].T * (w_ref[...] * factor)).astype(jnp.bfloat16)
 
     @pl.when(i >= n)
     def _():
-        prod = jnp.dot(v_ref[...], piece, preferred_element_type=jnp.float32)
-        u_ref[...] += lax.dot_general(
-            (prod * (root * root)).astype(jnp.bfloat16), piece, last,
-            preferred_element_type=jnp.float32)
+        for k in range(split):
+            prod = jnp.dot(v_ref[...], p_ref[k, 0], preferred_element_type=jnp.float32) * root(k)
+            u_ref[...] += spread(k, prod)
 
     @pl.when(i == 2 * n - 1)
     def _():
-        x = (q_ref[...] + factor * u_ref[...]).astype(jnp.bfloat16)
-        s_ref[...] = lax.dot_general(a_ref[...], x, last, preferred_element_type=jnp.float32)
+        x = (q_ref[...] + factor * u_ref[...].T).astype(jnp.bfloat16)
+        s_ref[...] = lax.dot_general(
+            a_ref[...], x, (((1,), (1,)), ((), ())), preferred_element_type=jnp.float32)
 
 
 def chi_and_screen(left, pieces, weight, coulomb_root):
     width, packed = left.shape
-    split, blocks, _, sub = pieces.shape
-    n = split * blocks
+    split, n, _, sub = pieces.shape
     return pl.pallas_call(
         functools.partial(chi_kernel, n, 8.0 / G),
         grid=(2 * n,),
         out_shape=(
-            jax.ShapeDtypeStruct((width, n * sub), jnp.bfloat16),
+            jax.ShapeDtypeStruct((width, n * split * sub), jnp.bfloat16),
             jax.ShapeDtypeStruct((width, CW), jnp.float32),
         ),
         in_specs=[
             pl.BlockSpec((width, packed), lambda i: (0, 0)),
-            pl.BlockSpec((1, 1, packed, sub), lambda i: (i % split, (i // split) % blocks, 0, 0)),
+            pl.BlockSpec((split, 1, packed, sub), lambda i: (0, i % n, 0, 0)),
             pl.BlockSpec((1, packed), lambda i: (0, 0)),
-            pl.BlockSpec((1, sub), lambda i: (0, i % n)),
+            pl.BlockSpec((1, split * sub), lambda i: (0, i % n)),
         ],
         out_specs=(
-            pl.BlockSpec((width, sub), lambda i: (0, jnp.minimum(i, n - 1))),
+            pl.BlockSpec((width, split * sub), lambda i: (0, jnp.minimum(i, n - 1))),
             pl.BlockSpec((width, CW), lambda i: (0, 0)),
         ),
         scratch_shapes=[
             pltpu.VMEM((width + CW, packed), jnp.bfloat16),
             pltpu.VMEM((CW, packed), jnp.float32),
-            pltpu.VMEM((CW, packed), jnp.float32),
+            pltpu.VMEM((packed, CW), jnp.float32),
             pltpu.VMEM((CW, packed), jnp.bfloat16),
         ],
         compiler_params=pltpu.CompilerParams(vmem_limit_bytes=48 * 1024 * 1024),
     )(left, pieces, weight[None, :], coulomb_root[None, :])
 
 
-def gather_kernel(nz, own_ref, out_ref, recv, s_up, s_down, s_y, s_x, s_pair, s_own):
+def gather_kernel(
+    nz, rows_ref, energy_ref, source_ref, out_ref, energies_ref,
+    all_ref, pick_ref, own_ref, recv, s_up, s_down, s_y, s_x, s_pair, s_own,
+    r_rows, s_rows, s_local, r_energy, s_energy,
+):
     g, b = lax.axis_index("grp"), lax.axis_index("blk")
     x, c = g // 2, g % 2
     z, y = b // 2, b % 2
@@ -213,10 +219,10 @@
         return copy(q, bb, s_pair.at[q, bb], to_pair)
 
     def takes_y(zz, j):
-        return (zz % 2 == 0) | (j != skip_y)
+        return (zz % 4 != 1) | (j != skip_y)
 
     def other_y_takes_x(zz, j):
-        return ((zz % 2 == 0) & (j == own_x)) | ((zz % 2 == 1) & (j != skip_y))
+        return ((zz % 4 != 1) & (j == own_x)) | ((zz % 4 == 1) & (j != skip_y))
 
     def when(condition, make, act):
         @pl.when(condition)
@@ -256,11 +262,11 @@
             def _():
                 take(3 * (1 - x))
         else:
-            @pl.when(valid & (zz % 2 == 0))
+            @pl.when(valid & (zz % 4 != 1))
             def _():
                 take(3 * (1 - x))
 
-            @pl.when(valid & (zz % 2 == 1))
+            @pl.when(valid & (zz % 4 == 1))
             def _():
                 take(2 * (1 - x))
                 take(2 * (1 - x) + 1)
@@ -282,12 +288,71 @@
     peers = 3 + has_up.astype(jnp.int32) + has_down.astype(jnp.int32)
     pl.semaphore_wait(barrier, peers)
 
-    for j in range(3):
-        when(has_up, lambda: up(z, j, True), "start")
-        when(has_down, lambda: down(z, j, True), "start")
-        when(takes_y(z, j), lambda: over_y(z, j, True), "start")
-    keep = pltpu.make_async_copy(own_ref, out_ref.at[:, b], s_own)
-    keep.start()
+    slots, packed, sub = rows_ref.shape[0], own_ref.shape[1], own_ref.shape[2]
+    g_x, g_pair = (1 - x) * 2 + c, x * 2 + 1 - c
+    g_far = (1 - x) * 2 + 1 - c
+
+    def span(k):
+        return pl.ds(pl.multiple_of(k * slots, slots), slots)
+
+    def order(j):
+        return jnp.where(j < 3, x + j, 3 * (1 - x))
+
+    def rows_to(q, way, to, who):
+        dst = all_ref.at[q, span(who)]
+        columns = pl.ds(pl.multiple_of(q * sub, sub), sub)
+        return pltpu.make_async_remote_copy(
+            src_ref=dst if way == 2 else rows_ref.at[:, columns], dst_ref=dst,
+            send_sem=s_rows.at[way, q], recv_sem=r_rows.at[q, who], device_id=to,
+            device_id_type=pl.DeviceIdType.MESH)
+
+    def rows_local(q):
+        columns = pl.ds(pl.multiple_of(q * sub, sub), sub)
+        return pltpu.make_async_copy(rows_ref.at[:, columns], all_ref.at[q, span(g)], s_local.at[q])
+
+    def energy_to(way, to, who):
+        return pltpu.make_async_remote_copy(
+            src_ref=energies_ref.at[who] if way == 2 else energy_ref.at[0],
+            dst_ref=energies_ref.at[who], send_sem=s_energy.at[way], recv_sem=r_energy.at[who],
+            device_id=to, device_id_type=pl.DeviceIdType.MESH)
+
+    for j in range(4):
+        q = order(j)
+        rows_to(q, 0, to_x, g).start()
+        rows_to(q, 1, to_pair, g).start()
+        rows_local(q).start()
+    energy_to(0, to_x, g).start()
+    energy_to(1, to_pair, g).start()
+    keep_energy = pltpu.make_async_copy(energy_ref.at[0], energies_ref.at[g], s_local.at[4])
+    keep_energy.start()
+
+    @pl.loop(0, packed // 128)
+    def _(k):
+        part = pl.ds(pl.multiple_of(k * 128, 128), 128)
+        at = lax.broadcasted_iota(jnp.int32, (128, pick_ref.shape[1]), 1)
+        pick_ref[part] = (source_ref[part] == at).astype(jnp.float32).astype(jnp.bfloat16)
+
+    def keep(q):
+        return pltpu.make_async_copy(own_ref.at[q], out_ref.at[q, b], s_own.at[q])
+
+    @pl.loop(0, 4)
+    def _(j):
+        q = order(j)
+        rows_to(q, 0, to_x, g_x).wait_recv()
+        rows_to(q, 2, to_pair, g_x).start()
+        rows_local(q).wait()
+        rows_to(q, 1, to_pair, g_pair).wait_recv()
+        rows_to(q, 2, to_pair, g_far).wait_recv()
+        own_ref[q] = jnp.dot(
+            pick_ref[...], all_ref[q], preferred_element_type=jnp.float32).astype(jnp.bfloat16)
+        carried = j < 3
+        when(carried & has_up, lambda: up(z, j, True), "start")
+        when(carried & has_down, lambda: down(z, j, True), "start")
+        when(carried & takes_y(z, j), lambda: over_y(z, j, True), "start")
+        keep(q).start()
+
+    energy_to(0, to_x, g_x).wait_recv()
+    energy_to(2, to_pair, g_x).start()
 
     for s in range(nz + 1):
         for j in range(3):
@@ -311,7 +376,18 @@
             device_id=to_pair, device_id_type=pl.DeviceIdType.MESH).wait_recv()
         over_pair(q, bb).wait_send()
 
-    keep.wait()
+    energy_to(1, to_pair, g_pair).wait_recv()
+    energy_to(2, to_pair, g_far).wait_recv()
+    energy_to(0, to_x, g).wait_send()
+    energy_to(1, to_pair, g).wait_send()
+    energy_to(2, to_pair, g_x).wait_send()
+    keep_energy.wait()
+    for j in range(4):
+        q = order(j)
+        rows_to(q, 0, to_x, g).wait_send()
+        rows_to(q, 1, to_pair, g).wait_send()
+        rows_to(q, 2, to_pair, g_x).wait_send()
+        keep(q).wait()
     for j in range(3):
         when(has_up, lambda: up(z, j, True), "wait_send")
         when(has_down, lambda: down(z, j, True), "wait_send")
@@ -334,23 +410,31 @@
                             lambda q=q: from_pair(q, zz * 2 + (y if same_y else 1 - y)))
 
 
-def gather_pieces(own, blocks):
-    split, packed, sub = own.shape
-    nz = blocks // 2
+def gather_pieces(pair_density, energies, source, blocks, split):
+    slots, width = pair_density.shape
+    packed = source.shape[0]
+    sub, nz = width // split, blocks // 2
     dma = pltpu.SemaphoreType.DMA
-    sent = 28 * packed * sub
+    vmem = pl.BlockSpec(memory_space=pltpu.VMEM)
     return pl.pallas_call(
         functools.partial(gather_kernel, nz),
-        out_shape=jax.ShapeDtypeStruct((split, blocks, packed, sub), own.dtype),
-        in_specs=[pl.BlockSpec(memory_space=pltpu.VMEM)],
-        out_specs=pl.BlockSpec(memory_space=pl.ANY),
+        out_shape=(
+            jax.ShapeDtypeStruct((split, blocks, packed, sub), jnp.bfloat16),
+            jax.ShapeDtypeStruct((split, 1, slots), jnp.float32),
+        ),
+        in_specs=[vmem, vmem, vmem],
+        out_specs=(pl.BlockSpec(memory_space=pl.ANY), vmem),
         scratch_shapes=[
+            pltpu.VMEM((split, split * slots, sub), jnp.bfloat16),
+            pltpu.VMEM((packed, split * slots), jnp.bfloat16),
+            pltpu.VMEM((split, packed, sub), jnp.bfloat16),
             dma((split, blocks, 2)), dma((3, nz)), dma((3, nz)), dma((3, nz)),
-            dma((3, blocks)), dma((split, blocks)), dma(()),
+            dma((3, blocks)), dma((split, blocks)), dma((split,)),
+            dma((split, split)), dma((3, split)), dma((split + 1,)), dma((split,)), dma((3,)),
         ],
-        compiler_params=pltpu.CompilerParams(collective_id=0, has_side_effects=True),
-        cost_estimate=pl.CostEstimate(flops=0, bytes_accessed=2 * sent, transcendentals=0),
-    )(own)
+        compiler_params=pltpu.CompilerParams(
+            collective_id=0, has_side_effects=True, vmem_limit_bytes=40 * 1024 * 1024),
+    )(pair_density, energies[None, None, :], source[:, None])
 
 
 def body(pair_density, energies, batch_live, coulomb_root):
@@ -363,22 +447,17 @@
     block_index = lax.axis_index("blk")
     own_root = lax.dynamic_slice_in_dim(coulomb_root, block_index * width, width)
 
-    rows = lax.all_gather(pair_density, "grp", axis=0, tiled=True)
-    all_energy = lax.all_gather(energies, "grp", axis=0, tiled=True)
     source, used = pack_rows(batch_live, slots, total, packed)
+    pieces, all_energy = gather_pieces(pair_density, energies, source, blocks, group_count)
     pick = source[:, None] == jnp.arange(total, dtype=jnp.int32)[None, :]
-    own = jnp.dot(pick.astype(jnp.bfloat16), rows, preferred_element_type=jnp.float32).astype(
-        jnp.bfloat16
-    )
-    energy = jnp.sum(jnp.where(pick, all_energy[None, :], 0.0), axis=1)
+    energy = jnp.sum(jnp.where(pick, jnp.reshape(all_energy, (1, total)), 0.0), axis=1)
     energy = jnp.where(used, energy, 1.0)
     frequency = 0.6 * group_index.astype(jnp.float32)
     weight = -2.0 * energy / (energy * energy + frequency * frequency)
     weight = jnp.where(used, weight, 0.0) * (1.0 / math.sqrt(total))
-    left = (own.T.astype(jnp.float32) * weight[None, :] * own_root[:, None]).astype(jnp.bfloat16)
-    quarters = jnp.transpose(
-        jnp.reshape(own, (packed, group_count, width // group_count)), (1, 0, 2))
-    pieces = gather_pieces(quarters, blocks)
+    own = lax.dynamic_index_in_dim(pieces, block_index, 1, keepdims=False)
+    own = jnp.reshape(jnp.swapaxes(own, 1, 2), (width, packed)).astype(jnp.float32)
+    left = (own * weight[None, :] * own_root[:, None]).astype(jnp.bfloat16)
     polarized, screened = chi_and_screen(left, pieces, weight, coulomb_root)
     return (polarized[None], screened[None])
 

time: 251 us -> 214 us (0.85)
  waiting for transfers between devices: 30 us -> 0 us
  between operations: 14.1 us -> 0.7 us
  matrix products: 8.4 us -> 0 us
  other arithmetic: 3.83 us -> 10.8 us
  blocking collectives: 6.32 us -> 0 us
  local copies, waits for them, and re-layouts: 2.68 us -> 8.78 us
  Pallas kernels: 185 us -> 191 us
    all_gather x1 -> x0, waiting for transfers between devices: 29.3 us -> none  [body(): rows = lax.all_gather(pair_density, 'grp', axis=0, tiled=True)]
    pallas_call x1, Pallas kernels: 101 us -> 114 us  [gather_pieces(): pl.pallas_call(functools.partial(gather_kernel, nz), out_shape=(jax.Shape...]
    dot_general x1 -> x0, matrix products: 8.4 us -> none  [body(): jnp.dot(pick.astype(jnp.bfloat16), rows, preferred_element_type=jnp.float32)]
    convert_element_type x0 -> x2, other arithmetic: none -> 7.57 us  [the longest x1 4.57 us: body(): jnp.reshape(jnp.swapaxes(own, 1, 2), (width, packed)).astype(jnp.float32)]
    pallas_call x1, Pallas kernels: 84.2 us -> 77.6 us  [chi_and_screen(): pl.pallas_call(functools.partial(chi_kernel, n, 8.0 / G), grid=(2 * n,),...]
    all_gather x1 -> x0, blocking collectives: 6.32 us -> none  [body(): all_energy = lax.all_gather(energies, 'grp', axis=0, tiled=True)]
    convert_element_type x0 -> x1, local copies, waits for them, and re-layouts: none -> 5.96 us  [body(): jnp.reshape(jnp.swapaxes(own, 1, 2), (width, packed)).astype(jnp.float32)]
    reshape x1 -> x0, local copies, waits for them, and re-layouts: 2.56 us -> none  [body(): jnp.reshape(own, (packed, group_count, width // group_count))]
  transfers between devices with their start and end apart: 1 -> 0, of which waited for: 1 -> 0; matrix products, arithmetic and copies ran while one was open for 1% -> 0% of each run, Pallas kernels for 0% -> 0%
where the time goes in v3:
time: 214 us; the launch traced here: 212 us
  Pallas kernels  191 us (89%)
  other arithmetic  10.8 us (5%)
  local copies, waits for them, and re-layouts  8.78 us (4%)
    pallas_call x1, Pallas kernels, gather_pieces(): pl.pallas_call(functools.partial(gather_kernel, nz), out_shape=(jax.Shape...  114 us
    pallas_call x1, Pallas kernels, chi_and_screen(): pl.pallas_call(functools.partial(chi_kernel, n, 8.0 / G), grid=(2 * n,),...  77.6 us
    convert_element_type x1, local copies, waits for them, and re-layouts, body(): jnp.reshape(jnp.swapaxes(own, 1, 2), (width, packed)).astype(jnp.float32)  5.96 us
    convert_element_type x1, other arithmetic, body(): jnp.reshape(jnp.swapaxes(own, 1, 2), (width, packed)).astype(jnp.float32)  4.57 us

profile of v3, /device:TPU:0, one launch (start us, length us, event | category | flops | bytes accessed | tf_op | source)
XLA Modules:
  0.0 211.7 jit_solution(9276429294444839434)
XLA Ops:
  0.6 0.8 reduce-window.8
  1.5 0.7 multiply_subtract_fusion
  2.1 0.1 fusion.4
  2.2 0.7 dynamic_slice.8
  2.9 0.1 select_reduce_fusion.1
  3.0 0.2 select_n.67.source_ref
  3.3 0.0 copy-start
  3.3 1.2 copy-done
  4.5 0.0 copy-start.2
  4.5 0.7 copy-done.2
  5.2 113.9 %shard_map.59 = (bf16[4,8,1280,256]{3,2,1,0:T(8,128)(2,1)}, f32[4,1,512]{2,1,0:T(1,128)S(1)}) custom-call(bf16[512,1024]{1,0:T(8,128)(2,1)S(1)} %copy-done, f32[1,1,512]{2,1,0:T(1,128)S(1)} %bitcast.21, s32[1280,1]{1,0:T(8,128)S(1)} %select_n.67.source_ref), custom_call_target="tpu_custom_call" | custom-call | tf_op jit(solution)/shard_map/pallas_call | solution.py:419
  119.0 1.5 select_reduce_fusion
  120.6 4.6 %convert_bitcast_fusion = f32[4,256,1280]{1,2,0:T(8,128)} fusion(bf16[4,8,1280,256]{3,2,1,0:T(8,128)(2,1)} %get-tuple-element.6.p_ref, s32[]{:T(128)S(6)} %select_n.60), kind=kLoop, calls=%fused_computation.2 | loop fusion | flops 1310720 | bytes 7864324 | tf_op jit(solution)/shard_map/convert_element_type | solution.py:459
  125.1 6.0 %copy.10 = f32[4,256,1280]{2,1,0:T(8,128)} copy(f32[4,256,1280]{1,2,0:T(8,128)} %convert_bitcast_fusion) | data formatting | bytes 10485760 | tf_op jit(solution)/shard_map/convert_element_type | solution.py:459
  131.1 0.0 copy-start.1
  131.1 3.0 %fusion.1.a_ref = bf16[1024,1280]{1,0:T(8,128)(2,1)S(1)} fusion(f32[4,256,1280]{2,1,0:T(8,128)} %copy.10, f32[1024]{0:T(1024)S(1)} %dynamic_slice.8, f32[1280]{0:T(1024)S(1)} %select_multiply_fusion), kind=kLoop, calls=%fused_computation.5 | loop fusion | flops 3932160 | bytes 7873536 | tf_op jit(solution)/shard_map/convert_element_type | solution.py:460
  134.1 0.0 copy-done.1
  134.1 77.6 %shard_map.60 = (bf16[1024,8192]{1,0:T(8,128)(2,1)}, f32[1024,128]{1,0:T(8,128)}) custom-call(bf16[1024,1280]{1,0:T(8,128)(2,1)S(1)} %fusion.1.a_ref, bf16[4,8,1280,256]{3,2,1,0:T(8,128)(2,1)} %get-tuple-element.6.p_ref, f32[1,1280]{1,0:T(1,128)S(1)} %fusion.3.w_ref, f32[1,8192]{1,0:T(1,128)S(1)} %bitcast.20), custom_call_target="tpu_custom_call" | custom-call | tf_op jit(solution)/shard_map/pallas_call | solution.py:152
  (3 shorter events, 0.0 us)
Async XLA Ops:
  3.3 1.2 copy-start
  4.5 0.7 copy-start.2
  131.1 3.0 %copy-start.1 = (f32[8192]{0:T(1024)S(1)}, f32[8192]{0:T(1024)}, u32[]{:S(2)}) copy-start(f32[8192]{0:T(1024)} %param.7) | copy-start | bytes 98308

commit v4 on v3

--- a/solution.py
+++ b/solution.py
@@ -102,9 +102,12 @@
     return source, used
 
 
-def chi_kernel(n, factor, a_ref, p_ref, w_ref, r_ref, out_ref, s_ref, at_ref, q_ref, u_ref, v_ref):
+def chi_kernel(
+    n, factor, own_ref, p_ref, w_ref, own_root_ref, r_ref, out_ref, s_ref,
+    at_ref, q_ref, u_ref, v_ref, t_ref,
+):
     i = pl.program_id(0)
-    width = a_ref.shape[0]
+    width = at_ref.shape[0] - CW
     split, _, _, sub = p_ref.shape
 
     def root(k):
@@ -116,7 +119,10 @@
 
     @pl.when(i == 0)
     def _():
-        at_ref[:width] = a_ref[...]
+        for k in range(split):
+            part = slice(k * sub, (k + 1) * sub)
+            left = (own_ref[k].astype(jnp.float32) * own_root_ref[:, part]).T
+            at_ref[part] = (left * w_ref[...]).astype(jnp.bfloat16)
         q = (p_ref[0, 0, :, :CW].astype(jnp.float32) * r_ref[:, :CW]).T
         q_ref[...] = q
         at_ref[width:] = (q * w_ref[...]).astype(jnp.bfloat16)
@@ -127,7 +133,12 @@
         for k in range(split):
             prod = jnp.dot(at_ref[...], p_ref[k, 0], preferred_element_type=jnp.float32) * root(k)
             out_ref[:, k * sub:(k + 1) * sub] = prod[:width].astype(jnp.bfloat16)
-            u_ref[...] += spread(k, prod[width:])
+            t_ref[:, k * sub:(k + 1) * sub] = prod[width:]
+
+    @pl.when(i < n)
+    def _():
+        for k in range(split):
+            u_ref[...] += spread(k, t_ref[:, k * sub:(k + 1) * sub])
 
     @pl.when(i == n - 1)
     def _():
@@ -143,12 +154,12 @@
     def _():
         x = (q_ref[...] + factor * u_ref[...].T).astype(jnp.bfloat16)
         s_ref[...] = lax.dot_general(
-            a_ref[...], x, (((1,), (1,)), ((), ())), preferred_element_type=jnp.float32)
-
-
-def chi_and_screen(left, pieces, weight, coulomb_root):
-    width, packed = left.shape
-    split, n, _, sub = pieces.shape
+            at_ref[:width], x, (((1,), (1,)), ((), ())), preferred_element_type=jnp.float32)
+
+
+def chi_and_screen(own, pieces, weight, own_root, coulomb_root):
+    split, n, packed, sub = pieces.shape
+    width = split * sub
     return pl.pallas_call(
         functools.partial(chi_kernel, n, 8.0 / G),
         grid=(2 * n,),
@@ -157,9 +168,10 @@
             jax.ShapeDtypeStruct((width, CW), jnp.float32),
         ),
         in_specs=[
-            pl.BlockSpec((width, packed), lambda i: (0, 0)),
+            pl.BlockSpec((split, packed, sub), lambda i: (0, 0, 0)),
             pl.BlockSpec((split, 1, packed, sub), lambda i: (0, i % n, 0, 0)),
             pl.BlockSpec((1, packed), lambda i: (0, 0)),
+            pl.BlockSpec((1, width), lambda i: (0, 0)),
             pl.BlockSpec((1, split * sub), lambda i: (0, i % n)),
         ],
         out_specs=(
@@ -171,14 +183,15 @@
             pltpu.VMEM((CW, packed), jnp.float32),
             pltpu.VMEM((packed, CW), jnp.float32),
             pltpu.VMEM((CW, packed), jnp.bfloat16),
+            pltpu.VMEM((CW, width), jnp.float32),
         ],
         compiler_params=pltpu.CompilerParams(vmem_limit_bytes=48 * 1024 * 1024),
-    )(left, pieces, weight[None, :], coulomb_root[None, :])
+    )(own, pieces, weight[None, :], own_root[None, :], coulomb_root[None, :])
 
 
 def gather_kernel(
-    nz, rows_ref, energy_ref, source_ref, out_ref, energies_ref,
-    all_ref, pick_ref, own_ref, recv, s_up, s_down, s_y, s_x, s_pair, s_own,
+    nz, rows_ref, energy_ref, source_ref, out_ref, energies_ref, own_ref,
+    all_ref, pick_ref, recv, s_up, s_down, s_y, s_x, s_pair, s_own,
     r_rows, s_rows, s_local, r_energy, s_energy,
 ):
     g, b = lax.axis_index("grp"), lax.axis_index("blk")
@@ -421,13 +434,13 @@
         out_shape=(
             jax.ShapeDtypeStruct((split, blocks, packed, sub), jnp.bfloat16),
             jax.ShapeDtypeStruct((split, 1, slots), jnp.float32),
+            jax.ShapeDtypeStruct((split, packed, sub), jnp.bfloat16),
         ),
         in_specs=[vmem, vmem, vmem],
-        out_specs=(pl.BlockSpec(memory_space=pl.ANY), vmem),
+        out_specs=(pl.BlockSpec(memory_space=pl.ANY), vmem, vmem),
         scratch_shapes=[
             pltpu.VMEM((split, split * slots, sub), jnp.bfloat16),
             pltpu.VMEM((packed, split * slots), jnp.bfloat16),
-            pltpu.VMEM((split, packed, sub), jnp.bfloat16),
             dma((split, blocks, 2)), dma((3, nz)), dma((3, nz)), dma((3, nz)),
             dma((3, blocks)), dma((split, blocks)), dma((split,)),
             dma((split, split)), dma((3, split)), dma((split + 1,)), dma((split,)), dma((3,)),
@@ -448,17 +461,14 @@
     own_root = lax.dynamic_slice_in_dim(coulomb_root, block_index * width, width)
 
     source, used = pack_rows(batch_live, slots, total, packed)
-    pieces, all_energy = gather_pieces(pair_density, energies, source, blocks, group_count)
+    pieces, all_energy, own = gather_pieces(pair_density, energies, source, blocks, group_count)
     pick = source[:, None] == jnp.arange(total, dtype=jnp.int32)[None, :]
     energy = jnp.sum(jnp.where(pick, jnp.reshape(all_energy, (1, total)), 0.0), axis=1)
     energy = jnp.where(used, energy, 1.0)
     frequency = 0.6 * group_index.astype(jnp.float32)
     weight = -2.0 * energy / (energy * energy + frequency * frequency)
     weight = jnp.where(used, weight, 0.0) * (1.0 / math.sqrt(total))
-    own = lax.dynamic_index_in_dim(pieces, block_index, 1, keepdims=False)
-    own = jnp.reshape(jnp.swapaxes(own, 1, 2), (width, packed)).astype(jnp.float32)
-    left = (own * weight[None, :] * own_root[:, None]).astype(jnp.bfloat16)
-    polarized, screened = chi_and_screen(left, pieces, weight, coulomb_root)
+    polarized, screened = chi_and_screen(own, pieces, weight, own_root, coulomb_root)
     return (polarized[None], screened[None])
 
 

time: 214 us -> 181 us (0.85)
  Pallas kernels: 191 us -> 172 us
  other arithmetic: 10.8 us -> 3.18 us
  local copies, waits for them, and re-layouts: 8.78 us -> 3.57 us
    pallas_call x1, Pallas kernels: 77.6 us -> 57.9 us  [chi_and_screen(): pl.pallas_call(functools.partial(chi_kernel, n, 8.0 / G), grid=(2 * n,),...]
    convert_element_type x2 -> x0, other arithmetic: 7.57 us -> none  [the longest x1 4.57 us: body(): jnp.reshape(jnp.swapaxes(own, 1, 2), (width, packed)).astype(jnp.float32)]
    convert_element_type x1 -> x0, local copies, waits for them, and re-layouts: 5.96 us -> none  [body(): jnp.reshape(jnp.swapaxes(own, 1, 2), (width, packed)).astype(jnp.float32)]
where the time goes in v4:
time: 181 us; the launch traced here: 179 us
  Pallas kernels  172 us (95%)
  local copies, waits for them, and re-layouts  3.57 us (2%)
  other arithmetic  3.18 us (2%)
    pallas_call x1, Pallas kernels, gather_pieces(): pl.pallas_call(functools.partial(gather_kernel, nz), out_shape=(jax.Shape...  114 us
    pallas_call x1, Pallas kernels, chi_and_screen(): pl.pallas_call(functools.partial(chi_kernel, n, 8.0 / G), grid=(2 * n,),...  57.9 us

profile of v4, /device:TPU:0, one launch (start us, length us, event | category | flops | bytes accessed | tf_op | source)
XLA Modules:
  0.0 179.2 jit_solution(2429892974477312134)
XLA Ops:
  0.6 0.8 reduce-window.8
  1.5 0.7 multiply_subtract_fusion
  2.1 0.1 fusion.2
  2.2 0.7 dynamic_slice.3
  2.9 0.1 select_reduce_fusion.1
  3.0 0.2 select_n.54.source_ref
  3.3 0.0 copy-start
  3.3 1.2 copy-done
  4.5 0.0 copy-start.2
  4.5 0.7 copy-done.2
  5.2 113.9 %shard_map.59 = (bf16[4,8,1280,256]{3,2,1,0:T(8,128)(2,1)}, f32[4,1,512]{2,1,0:T(1,128)S(1)}, bf16[4,1280,256]{2,1,0:T(8,128)(2,1)S(1)}) custom-call(bf16[512,1024]{1,0:T(8,128)(2,1)S(1)} %copy-done, f32[1,1,512]{2,1,0:T(1,128)S(1)} %bitcast.12, s32[1280,1]{1,0:T(8,128)S(1)} %select_n.54.source_ref), custom_call_target="tpu_custom_call" | custom-call | tf_op jit(solution)/shard_map/pallas_call | solution.py:432
  119.0 1.5 select_reduce_fusion
  120.5 0.0 copy-start.1
  120.5 0.7 copy-done.1
  121.3 57.9 %shard_map.60 = (bf16[1024,8192]{1,0:T(8,128)(2,1)}, f32[1024,128]{1,0:T(8,128)}) custom-call(bf16[4,1280,256]{2,1,0:T(8,128)(2,1)S(1)} %get-tuple-element.7.own_ref, bf16[4,8,1280,256]{3,2,1,0:T(8,128)(2,1)} %get-tuple-element.8.p_ref, f32[1,1280]{1,0:T(1,128)S(1)} %fusion.1.w_ref, f32[1,1024]{1,0:T(1,128)S(1)} %bitcast.11, f32[1,8192]{1,0:T(1,128)S(1)} %bitcast.10), custom_call_target="tpu_custom_call" | custom-call | tf_op jit(solution)/shard_map/pallas_call | solution.py:163
  (2 shorter events, 0.0 us)
Async XLA Ops:
  3.3 1.2 copy-start
  4.5 0.7 copy-start.2
  120.5 0.8 copy-start.1

commit v5 on v4

--- a/solution.py
+++ b/solution.py
@@ -232,10 +232,10 @@
         return copy(q, bb, s_pair.at[q, bb], to_pair)
 
     def takes_y(zz, j):
-        return (zz % 4 != 1) | (j != skip_y)
+        return (zz % 2 == 0) | (j != skip_y)
 
     def other_y_takes_x(zz, j):
-        return ((zz % 4 != 1) & (j == own_x)) | ((zz % 4 == 1) & (j != skip_y))
+        return ((zz % 2 == 0) & (j == own_x)) | ((zz % 2 == 1) & (j != skip_y))
 
     def when(condition, make, act):
         @pl.when(condition)
@@ -275,11 +275,11 @@
             def _():
                 take(3 * (1 - x))
         else:
-            @pl.when(valid & (zz % 4 != 1))
+            @pl.when(valid & (zz % 2 == 0))
             def _():
                 take(3 * (1 - x))
 
-            @pl.when(valid & (zz % 4 == 1))
+            @pl.when(valid & (zz % 2 == 1))
             def _():
                 take(2 * (1 - x))
                 take(2 * (1 - x) + 1)
@@ -367,7 +367,7 @@
     energy_to(0, to_x, g_x).wait_recv()
     energy_to(2, to_pair, g_x).start()
 
-    for s in range(nz + 1):
+    for s in range(nz + 2):
         for j in range(3):
             if 1 <= s + 1 < nz:
                 for zz, below, valid in at_distance(s + 1):
@@ -375,11 +375,11 @@
             if s < nz:
                 for zz, _, valid in at_distance(s):
                     from_y(zz, j, valid)
-        if 1 <= s < nz:
-            for zz, _, valid in at_distance(s):
+        if 2 <= s <= nz:
+            for zz, _, valid in at_distance(s - 1):
                 from_x(zz, True, valid)
-        if s >= 1:
-            for zz, _, valid in at_distance(s - 1):
+        if s >= 2:
+            for zz, _, valid in at_distance(s - 2):
                 from_x(zz, False, valid)
 
     def from_pair(q, bb):

time: 181 us -> 184 us (1.017)
  Pallas kernels: 172 us -> 176 us
    pallas_call x1, Pallas kernels: 114 us -> 118 us  [gather_pieces(): pl.pallas_call(functools.partial(gather_kernel, nz), out_shape=(jax.Shape...]
where the time goes in v5:
time: 184 us; the launch traced here: 183 us
  Pallas kernels  176 us (96%)
  local copies, waits for them, and re-layouts  3.57 us (2%)
  other arithmetic  3.18 us (2%)
    pallas_call x1, Pallas kernels, gather_pieces(): pl.pallas_call(functools.partial(gather_kernel, nz), out_shape=(jax.Shape...  118 us
    pallas_call x1, Pallas kernels, chi_and_screen(): pl.pallas_call(functools.partial(chi_kernel, n, 8.0 / G), grid=(2 * n,),...  57.9 us

profile of v5, /device:TPU:0, one launch (start us, length us, event | category | flops | bytes accessed | tf_op | source)
XLA Modules:
  0.0 183.3 jit_solution(5517478093651985387)
XLA Ops:
  0.6 0.8 reduce-window.8
  1.5 0.7 multiply_subtract_fusion
  2.1 0.1 fusion.2
  2.2 0.7 dynamic_slice.3
  2.9 0.1 select_reduce_fusion.1
  3.0 0.2 select_n.54.source_ref
  3.3 0.0 copy-start
  3.3 1.2 copy-done
  4.5 0.0 copy-start.2
  4.5 0.7 copy-done.2
  5.2 118.1 %shard_map.59 = (bf16[4,8,1280,256]{3,2,1,0:T(8,128)(2,1)}, f32[4,1,512]{2,1,0:T(1,128)S(1)}, bf16[4,1280,256]{2,1,0:T(8,128)(2,1)S(1)}) custom-call(bf16[512,1024]{1,0:T(8,128)(2,1)S(1)} %copy-done, f32[1,1,512]{2,1,0:T(1,128)S(1)} %bitcast.12, s32[1280,1]{1,0:T(8,128)S(1)} %select_n.54.source_ref), custom_call_target="tpu_custom_call" | custom-call | tf_op jit(solution)/shard_map/pallas_call | solution.py:432
  123.2 1.5 select_reduce_fusion
  124.7 0.0 copy-start.1
  124.7 0.7 copy-done.1
  125.5 57.9 %shard_map.60 = (bf16[1024,8192]{1,0:T(8,128)(2,1)}, f32[1024,128]{1,0:T(8,128)}) custom-call(bf16[4,1280,256]{2,1,0:T(8,128)(2,1)S(1)} %get-tuple-element.7.own_ref, bf16[4,8,1280,256]{3,2,1,0:T(8,128)(2,1)} %get-tuple-element.8.p_ref, f32[1,1280]{1,0:T(1,128)S(1)} %fusion.1.w_ref, f32[1,1024]{1,0:T(1,128)S(1)} %bitcast.11, f32[1,8192]{1,0:T(1,128)S(1)} %bitcast.10), custom_call_target="tpu_custom_call" | custom-call | tf_op jit(solution)/shard_map/pallas_call | solution.py:163
  (2 shorter events, 0.0 us)
Async XLA Ops:
  3.3 1.2 copy-start
  4.5 0.7 copy-start.2
  124.7 0.8 copy-start.1

commit v6 on v4

--- a/solution.py
+++ b/solution.py
@@ -205,7 +205,7 @@
     to_x = ((1 - x) * 2 + c, b)
     to_pair = (x * 2 + 1 - c, b)
     has_up, has_down = z + 1 < nz, z >= 1
-    skip_y, own_x = 2 * (1 - x), 2 * x
+    own_x = 2 * x
 
     def copy(q, bb, sem, to, own=False):
         src = own_ref.at[q, rows] if own else out_ref.at[q, bb, rows]
@@ -232,10 +232,10 @@
         return copy(q, bb, s_pair.at[q, bb], to_pair)
 
     def takes_y(zz, j):
-        return (zz % 4 != 1) | (j != skip_y)
+        return zz >= 0
 
     def other_y_takes_x(zz, j):
-        return ((zz % 4 != 1) & (j == own_x)) | ((zz % 4 == 1) & (j != skip_y))
+        return (zz >= 0) & (j == own_x)
 
     def when(condition, make, act):
         @pl.when(condition)
@@ -270,19 +270,9 @@
             arrived(q, bb)
             over_pair(q, bb).start()
 
-        if same_y:
-            @pl.when(valid)
-            def _():
-                take(3 * (1 - x))
-        else:
-            @pl.when(valid & (zz % 4 != 1))
-            def _():
-                take(3 * (1 - x))
-
-            @pl.when(valid & (zz % 4 == 1))
-            def _():
-                take(2 * (1 - x))
-                take(2 * (1 - x) + 1)
+        @pl.when(valid)
+        def _():
+            take(3 * (1 - x))
 
     def at_distance(d):
         if d == 0:

time: 181 us -> 186 us (1.028); the launches traced: 179 us -> 186 us
  Pallas kernels: 172 us -> 179 us
    pallas_call x1, Pallas kernels: 114 us -> 121 us  [gather_pieces(): pl.pallas_call(functools.partial(gather_kernel, nz), out_shape=(jax.Shape...]
where the time goes in v6:
time: 186 us
  Pallas kernels  179 us (96%)
  local copies, waits for them, and re-layouts  3.57 us (2%)
  other arithmetic  3.18 us (2%)
    pallas_call x1, Pallas kernels, gather_pieces(): pl.pallas_call(functools.partial(gather_kernel, nz), out_shape=(jax.Shape...  121 us
    pallas_call x1, Pallas kernels, chi_and_screen(): pl.pallas_call(functools.partial(chi_kernel, n, 8.0 / G), grid=(2 * n,),...  57.9 us

profile of v6, /device:TPU:0, one launch (start us, length us, event | category | flops | bytes accessed | tf_op | source)
XLA Modules:
  0.0 186.2 jit_solution(10605673093719337718)
XLA Ops:
  0.6 0.8 reduce-window.8
  1.5 0.7 multiply_subtract_fusion
  2.1 0.1 fusion.2
  2.2 0.7 dynamic_slice.3
  2.9 0.1 select_reduce_fusion.1
  3.0 0.2 select_n.54.source_ref
  3.3 0.0 copy-start
  3.3 1.2 copy-done
  4.5 0.0 copy-start.2
  4.5 0.7 copy-done.2
  5.2 120.9 %shard_map.59 = (bf16[4,8,1280,256]{3,2,1,0:T(8,128)(2,1)}, f32[4,1,512]{2,1,0:T(1,128)S(1)}, bf16[4,1280,256]{2,1,0:T(8,128)(2,1)S(1)}) custom-call(bf16[512,1024]{1,0:T(8,128)(2,1)S(1)} %copy-done, f32[1,1,512]{2,1,0:T(1,128)S(1)} %bitcast.12, s32[1280,1]{1,0:T(8,128)S(1)} %select_n.54.source_ref), custom_call_target="tpu_custom_call" | custom-call | tf_op jit(solution)/shard_map/pallas_call | solution.py:422
  126.1 1.5 select_reduce_fusion
  127.6 0.0 copy-start.1
  127.6 0.7 copy-done.1
  128.3 57.9 %shard_map.60 = (bf16[1024,8192]{1,0:T(8,128)(2,1)}, f32[1024,128]{1,0:T(8,128)}) custom-call(bf16[4,1280,256]{2,1,0:T(8,128)(2,1)S(1)} %get-tuple-element.7.own_ref, bf16[4,8,1280,256]{3,2,1,0:T(8,128)(2,1)} %get-tuple-element.8.p_ref, f32[1,1280]{1,0:T(1,128)S(1)} %fusion.1.w_ref, f32[1,1024]{1,0:T(1,128)S(1)} %bitcast.11, f32[1,8192]{1,0:T(1,128)S(1)} %bitcast.10), custom_call_target="tpu_custom_call" | custom-call | tf_op jit(solution)/shard_map/pallas_call | solution.py:163
  (2 shorter events, 0.0 us)
Async XLA Ops:
  3.3 1.2 copy-start
  4.5 0.7 copy-start.2
  127.6 0.8 copy-start.1
